TPU v7x, 32 devices: a whole 2x2x4 slice. The times are simulated.
32 devices in a mesh: leaf: 8 (over z, y), front: 4 (over x, core).
Axes of the slice: x: 2, y: 2, z: 4, core: 2. Of those that a mesh axis runs over, the one named last changes fastest.
Arguments:
- rhs_local: float32 [256, 256, 256], P(('leaf', 'front')), may hold values from -6 to 6
- dinv_local: float32 [256, 256, 256], P(('leaf', 'front')), may hold values from -1 to 2
- update_local: float32 [256, 256, 256], P(('leaf', 'front')), may hold values from -0.25 to 0.25
- parent: int32 [256], P(('leaf', 'front')), may hold values from 1 to 8, as said below
- row_blocks: int32 [256, 256], P(('leaf', 'front')), may hold values from 0 to 255, each once within a row
- sep_rhs: float32 [2048, 256], P(('leaf', 'front')), may hold values from -6 to 6
- sep_dinv: float32 [2048, 256], P(('leaf', 'front')), may hold values from -1 to 2
- sep_coupling: float32 [2048, 256], P(('leaf', 'front')), may hold values from -2 to 1
Outputs:
- sol_local: float32 [256, 256, 256], P(('leaf', 'front'))
- sep_solution: float32 [2048, 256], P(('leaf', 'front'))
Inputs may be any that keep to these rules, and one draw needn't show every extreme that they name: parent_k is the position of supernode k's parent within the same block of 8, always greater than k; the value 8 names the block's separator. `row_blocks`: each row is a permutation of 0 .. 255.
All inputs are finite; a program needn't handle non-finite values.
Results may differ from a plain program's by a relative error of at most 0.00024.
Values sent between devices are 32-bit elements; how exact they have to be, the bound alone decides.
No kernel may reach another device: no remote copies, remote signals or barrier semaphores. Data moves between devices by JAX's collectives and lax.ppermute only.
A program may use at most 128 MiB of HBM per device.

v0:
```python
import jax
import jax.numpy as jnp
from jax import lax
from jax.sharding import PartitionSpec as P


def entering(part, axis, combine, identity, reverse):
    count = lax.axis_size(axis)
    place = lax.axis_index(axis)
    ahead = count - 1 - place if reverse else place
    gathered = jax.tree.map(lambda a: lax.all_gather(a, axis), part)
    state = jax.tree.map(lambda a, e: jnp.zeros_like(a) + jnp.asarray(e, a.dtype), part, identity)

    def one(lap, state):
        source = count - 1 - lap if reverse else lap
        return combine(
            state, jax.tree.map(lambda a: lax.dynamic_index_in_dim(a, source, 0, False), gathered)
        )

    return lax.fori_loop(0, ahead, one, state)


def matmul(left, right):
    return jnp.dot(left, right, preferred_element_type=jnp.float32, precision=lax.Precision.HIGHEST)


def matmul_t(left, right):
    return lax.dot_general(
        left,
        right,
        (((0,), (0,)), ((), ())),
        precision=lax.Precision.HIGHEST,
        preferred_element_type=jnp.float32,
    )


def compose_ahead(earlier, latter):
    return (matmul(latter[0], earlier[0]), matmul(latter[0], earlier[1]) + latter[1])


def compose_back(earlier, latter):
    return (matmul(earlier[0], latter[0]), matmul_t(latter[0], earlier[1]) + latter[1])


def forward_block(rhs_block, inverse, update, parent_block, row_index):
    count_nodes = rhs_block.shape[0]
    pending = jnp.zeros((count_nodes + 1,) + rhs_block.shape[1:], jnp.float32)
    finished_solution = jnp.zeros(rhs_block.shape, jnp.float32)

    def advance(step_no, state_pair):
        pending_rows, finished_rows = state_pair
        solved_node = matmul(inverse[step_no], rhs_block[step_no] - pending_rows[step_no])
        update_rows = jnp.take(matmul(update[step_no], solved_node), row_index[step_no], axis=0)
        pending_rows = pending_rows.at[parent_block[step_no]].add(update_rows)
        return (pending_rows, finished_rows.at[step_no].set(solved_node))

    pending, finished_solution = lax.fori_loop(
        0, count_nodes, advance, (pending, finished_solution)
    )
    return (finished_solution, pending[count_nodes])


def backward_block(finished_solution, inverse, update, parent_block, row_index, top_value):
    count_nodes = finished_solution.shape[0]
    known_rows = jnp.concatenate(
        [jnp.zeros(finished_solution.shape, jnp.float32), top_value[None]], axis=0
    )

    def retreat(step_no, known_state):
        node_pos = count_nodes - 1 - step_no
        parent_value = known_state[parent_block[node_pos]]
        placed = (
            jnp.zeros(parent_value.shape, jnp.float32).at[row_index[node_pos]].set(parent_value)
        )
        result = matmul_t(
            inverse[node_pos], finished_solution[node_pos] - matmul_t(update[node_pos], placed)
        )
        return known_state.at[node_pos].set(result)

    known_rows = lax.fori_loop(0, count_nodes, retreat, known_rows)
    return known_rows[:count_nodes]


def local(rhs_local, dinv_local, update_local, parent, row_blocks, sep_rhs, sep_dinv, sep_coupling):
    finished_solution, top_term = forward_block(
        rhs_local, dinv_local, update_local, parent, row_blocks
    )
    front_pos = lax.axis_index("front")
    share_rows = sep_rhs.shape[0]
    block_order = sep_dinv.shape[1]
    drive_share = sep_rhs - lax.psum_scatter(top_term, "front", scatter_dimension=0, tiled=True)
    coupling, drive_full = (
        lax.all_gather(sep_coupling, "front", axis=0, tiled=True),
        lax.all_gather(drive_share, "front", axis=0, tiled=True),
    )
    chain_map, drive_term = (
        lax.all_gather(-matmul(sep_dinv, coupling), "front", axis=0, tiled=True),
        lax.all_gather(matmul(sep_dinv, drive_full), "front", axis=0, tiled=True),
    )
    unit_map = jnp.eye(block_order, dtype=jnp.float32)
    previous = entering(
        (chain_map, drive_term),
        "leaf",
        compose_ahead,
        (unit_map, jnp.zeros_like(drive_term)),
        False,
    )[1]
    forward_top = matmul(chain_map, previous) + drive_term
    back_drive = -matmul_t(chain_map, forward_top)
    following = entering(
        (chain_map, back_drive), "leaf", compose_back, (unit_map, jnp.zeros_like(back_drive)), True
    )[1]
    residue = forward_top - following
    own_residue = lax.dynamic_slice_in_dim(residue, front_pos * share_rows, share_rows, 0)
    top_value = lax.psum(matmul_t(sep_dinv, own_residue), "front")
    sep_solution = lax.dynamic_slice_in_dim(top_value, front_pos * share_rows, share_rows, 0)
    sol_local = backward_block(
        finished_solution, dinv_local, update_local, parent, row_blocks, top_value
    )
    return (sol_local, sep_solution)


def solution(mesh):
    placed = (
        P(("leaf", "front"), None, None),
        P(("leaf", "front"), None, None),
        P(("leaf", "front"), None, None),
        P(("leaf", "front")),
        P(("leaf", "front"), None),
        P(("leaf", "front"), None),
        P(("leaf", "front"), None),
        P(("leaf", "front"), None),
    )
    return jax.shard_map(
        local,
        mesh=mesh,
        in_specs=placed,
        out_specs=(P(("leaf", "front"), None, None), P(("leaf", "front"), None)),
        check_vma=False,
    )
```

profile of v0, /device:TPU:0, one launch (start us, length us, event | category | flops | bytes accessed | tf_op | source)
XLA Modules:
  0.0 391.7 jit_solution(16533572137065074752)
XLA Ops:
  9.8 79.2 %while.59 = (s32[]{:T(128)}, f32[9,256,256]{2,1,0:T(8,128)S(1)}, f32[8,256,256]{2,1,0:T(8,128)}, s32[8]{0:T(128)S(1)}, s32[8,256]{1,0:T(8,128)}, /*index=5*/f32[...) while((s32[]{:T(128)}, f32[9,256,256]{2,1,0:T(8,128)S(1)}, ...), condition=%wide.region_3.4_spmd, body=%wide.region_0.3_spmd.sunk | while | flops 402984224 | bytes 3683810 | solution.py:57
  13.1 2.8 fusion.67
  23.0 2.8 fusion.67
  32.9 2.8 fusion.67
  42.8 2.8 fusion.67
  52.7 2.8 fusion.67
  62.6 2.8 fusion.67
  72.5 2.8 fusion.67
  82.4 2.8 fusion.67
  89.9 7.2 %all_gather.32 = f32[256,256]{1,0:T(8,128)S(1)} all-gather(f32[64,256]{1,0:T(8,128)S(1)} %copy-done.3), channel_id=1, replica_groups=mesh['leaf'=8,'front'=4] {'front'}, dimensions={0}, use_global_device_ids=true | all-gather | bytes 327680 | tf_op jit(solution)/shard_map/all_gather | solution.py:93
  97.3 6.3 %all_gather.33 = f32[256,256]{1,0:T(8,128)} all-gather(f32[64,256]{1,0:T(8,128)S(1)} %convolution_negate_fusion.1), channel_id=1, replica_groups=mesh['leaf'=8,'front'=4] {'front'}, dimensions={0}, use_global_device_ids=true | all-gather | bytes 327680 | tf_op jit(solution)/shard_map/all_gather | solution.py:97
  103.7 9.0 %reduce-scatter.2.cloned.1.call-done = f32[64,256]{1,0:T(8,128)} async-done(((f32[256,256]{1,0:T(8,128)}), f32[64,256]{1,0:T(8,128)}) %reduce-scatter.2.cloned.1.call-update) | async-done | bytes 65552 | tf_op jit(solution)/shard_map/reduce_scatter | solution.py:91
  113.5 5.8 %all_gather.36 = f32[256,256]{1,0:T(8,128)S(1)} all-gather(f32[64,256]{1,0:T(8,128)S(1)} %sub.46), channel_id=1, replica_groups=mesh['leaf'=8,'front'=4] {'front'}, dimensions={0}, use_global_device_ids=true | all-gather | bytes 327680 | tf_op jit(solution)/shard_map/all_gather | solution.py:94
  119.6 6.3 %all_gather.37 = f32[256,256]{1,0:T(8,128)} all-gather(f32[64,256]{1,0:T(8,128)S(1)} %convolution_bitcast_fusion.2), channel_id=1, replica_groups=mesh['leaf'=8,'front'=4] {'front'}, dimensions={0}, use_global_device_ids=true | all-gather | bytes 327680 | tf_op jit(solution)/shard_map/all_gather | solution.py:98
  126.0 28.4 %all-gather.7.cloned.1.call-done = f32[2048,256]{1,0:T(8,128)} async-done(((f32[256,256]{1,0:T(8,128)}), f32[2048,256]{1,0:T(8,128)}) %all-gather.7.cloned.1.call-update) | async-done | bytes 2097168 | tf_op jit(solution)/shard_map/all_gather | solution.py:11
  154.4 49.9 %all-gather.9.cloned.1.call-done = f32[2048,256]{1,0:T(8,128)} async-done(((f32[256,256]{1,0:T(8,128)}), f32[2048,256]{1,0:T(8,128)}) %all-gather.9.cloned.1.call-update) | async-done | bytes 2097168 | tf_op jit(solution)/shard_map/all_gather | solution.py:11
  207.2 57.1 %all-gather.11.cloned.1.call-done = f32[2048,256]{1,0:T(8,128)} async-done(((f32[256,256]{1,0:T(8,128)}), f32[2048,256]{1,0:T(8,128)}) %all-gather.11.cloned.1.call-update) | async-done | bytes 2097168 | tf_op jit(solution)/shard_map/all_gather | solution.py:11
  264.3 11.9 %while.61 = (s32[]{:T(128)}, f32[256,256]{1,0:T(8,128)S(1)}, s32[]{:T(128)}, f32[8,256,256]{2,1,0:T(8,128)}, f32[8,256,256]{2,1,0:T(8,128)}, /*index=5*/s32[]{:T(128)}, s32[]{:T(128)}, s32[]{:T(128)}, s32[]{:T(128)}) while((s32[]{:T(128)}, f32[256,256]{1,0:T(8,128)S(1)}, s32[]{:T(128)}, f32[8,256,256]{2,1,0:T(8,128)}, ...), condition=%wide.region_8.9_spmd, body=%wide.region_7.8_spmd.sunk | while | flops 201392128 | bytes 1574027 | solution.py:20
  277.4 29.3 %all-reduce.3.cloned.1.call-done = f32[256,256]{0,1:T(8,128)} async-done(((f32[256,256]{0,1:T(8,128)}), f32[256,256]{0,1:T(8,128)}) %all-reduce.3.cloned.1.call-update) | async-done | bytes 262160 | tf_op jit(solution)/shard_map/psum | solution.py:115
  309.7 72.8 %while.62 = (s32[]{:T(128)}, f32[9,256,256]{2,1,0:T(8,128)S(1)}, f32[8,256,256]{2,1,0:T(8,128)}, f32[8,256,256]{2,1,0:T(8,128)}, f32[8,256,256]{2,1,0:T(8,128)},...) while((s32[]{:T(128)}, f32[9,256,256]{2,1,0:T(8,128)S(1)}, ...), condition=%wide.region_13.14_spmd, body=%wide.region_10.13_spmd.sunk | while | flops 402785056 | bytes 2625843 | solution.py:80
  316.6 2.2 fusion.80
  343.9 2.2 fusion.80
  362.1 2.2 fusion.80
  371.2 2.2 fusion.80
  (165 shorter events, 115.3 us)
Async XLA Ops:
  8.0 89.1 %copy-start = (f32[64,256]{1,0:T(8,128)S(1)}, f32[64,256]{1,0:T(8,128)}, u32[]{:S(2)}) copy-start(f32[64,256]{1,0:T(8,128)} %param.28) | copy-start | bytes 196612
  8.0 104.7 %reduce-scatter.2.cloned.1.call-start = ((), (), s32[]{:S(2)}) async-start(), calls=%async_computation.1 | async-start | bytes 327680 | tf_op jit(solution)/shard_map/reduce_scatter | solution.py:91
  8.1 1.7 copy-start.5
  8.1 1.7 copy-start.6
  8.1 1.7 copy-start.7
  9.8 80.1 %copy-start.3 = (f32[64,256]{1,0:T(8,128)S(1)}, f32[64,256]{1,0:T(8,128)}, u32[]{:S(2)}) copy-start(f32[64,256]{1,0:T(8,128)} %param.29) | copy-start | bytes 196612
  89.1 23.6 %copy-start.4 = (f32[64,256]{1,0:T(8,128)S(1)}, f32[64,256]{1,0:T(8,128)}, u32[]{:S(2)}) copy-start(f32[64,256]{1,0:T(8,128)} %param.27) | copy-start | bytes 196612
  89.8 64.6 %all-gather.7.cloned.1.call-start = ((), (), s32[]{:S(2)}) async-start(), calls=%async_computation.3 | async-start | bytes 2359296 | tf_op jit(solution)/shard_map/all_gather | solution.py:11
  103.7 100.7 %all-gather.9.cloned.1.call-start = ((), (), s32[]{:S(2)}) async-start(), calls=%async_computation.4 | async-start | bytes 2359296 | tf_op jit(solution)/shard_map/all_gather | solution.py:11
  125.9 138.4 %all-gather.11.cloned.1.call-start = ((), (), s32[]{:S(2)}) async-start(), calls=%async_computation.5 | async-start | bytes 2359296 | tf_op jit(solution)/shard_map/all_gather | solution.py:11
  204.4 1.0 copy-start.1
  204.4 1.0 copy-start.2
  207.1 99.6 %all-reduce.3.cloned.1.call-start = ((), (), s32[]{:S(2)}) async-start(), calls=%async_computation.2 | async-start | bytes 524288 | tf_op jit(solution)/shard_map/psum | solution.py:115
Sparse Core Ops, SparseCore 0:
  89.9 22.7 reduce-scatter.1
  277.5 29.1 all-reduce.2
Sparse Core Ops, SparseCore 1:
  103.7 50.6 all-gather.6
  156.6 47.7 all-gather.8
  207.2 57.1 all-gather.10
where the time goes:
time: 394 us; the launch traced here: 392 us
  waiting for transfers between devices  174 us (44%)
  matrix products  78.4 us (20%)
  local copies, waits for them, and re-layouts  37.6 us (10%)
  other arithmetic  30.3 us (8%)
  loops' own time  29.8 us (8%)
  blocking collectives  25.6 us (6%)
  between operations  15.8 us (4%)
    all_gather x3, waiting for transfers between devices, entering(): gathered = jax.tree.map(lambda a: lax.all_gather(a, axis), part)  136 us
    dot_general x25, matrix products, matmul_t(): lax.dot_general(left, right, (((0,), (0,)), ((), ())), precision=lax.Prec...  44.3 us
    dot_general x19, matrix products, matmul(): jnp.dot(left, right, preferred_element_type=jnp.float32, precision=lax.Pr...  34.1 us
    psum x1, waiting for transfers between devices, local(): top_value = lax.psum(matmul_t(sep_dinv, own_residue), 'front')  29.3 us
    another operation x1, loops' own time, forward_block(): lax.fori_loop(0, count_nodes, advance, (pending, finished_solution))  15.5 us
    another operation x1, loops' own time, backward_block(): known_rows = lax.fori_loop(0, count_nodes, retreat, known_rows)  14 us
    another operation x16, other arithmetic  12.1 us
    scatter x8, local copies, waits for them, and re-layouts, retreat(): jnp.zeros(parent_value.shape, jnp.float32).at[row_index[node_pos]]  12 us
  transfers between devices with their start and end apart: 5, of which 5 were waited for; matrix products, arithmetic and copies ran while one was open for 0% of the time, Pallas kernels for 0%

commit v1 on v0

--- a/solution.py
+++ b/solution.py
@@ -82,6 +82,11 @@
 
 
 def local(rhs_local, dinv_local, update_local, parent, row_blocks, sep_rhs, sep_dinv, sep_coupling):
+
+    def shapes_produce(load):
+        new = jnp.sum(jax.lax.all_gather(load, axis_name="front"), 0)
+        return new
+
     finished_solution, top_term = forward_block(
         rhs_local, dinv_local, update_local, parent, row_blocks
     )
@@ -112,7 +117,7 @@
     )[1]
     residue = forward_top - following
     own_residue = lax.dynamic_slice_in_dim(residue, front_pos * share_rows, share_rows, 0)
-    top_value = lax.psum(matmul_t(sep_dinv, own_residue), "front")
+    top_value = shapes_produce(matmul_t(sep_dinv, own_residue))
     sep_solution = lax.dynamic_slice_in_dim(top_value, front_pos * share_rows, share_rows, 0)
     sol_local = backward_block(
         finished_solution, dinv_local, update_local, parent, row_blocks, top_value

time: 394 us -> 379 us (0.962)
  waiting for transfers between devices: 174 us -> 159 us
    psum x1 -> x0, waiting for transfers between devices: 29.3 us -> none  [local(): top_value = lax.psum(matmul_t(sep_dinv, own_residue), 'front')]
    all_gather x0 -> x1, waiting for transfers between devices: none -> 14.1 us  [shapes_produce(): new = jnp.sum(jax.lax.all_gather(load, axis_name='front'), 0)]
where the time goes in v1:
time: 379 us; the launch traced here: 377 us
  waiting for transfers between devices  159 us (42%)
  matrix products  78.4 us (21%)
  local copies, waits for them, and re-layouts  37.5 us (10%)
  other arithmetic  30.9 us (8%)
  loops' own time  29.8 us (8%)
  blocking collectives  25.6 us (7%)
  between operations  15.9 us (4%)
    all_gather x3, waiting for transfers between devices, entering(): gathered = jax.tree.map(lambda a: lax.all_gather(a, axis), part)  136 us
    dot_general x25, matrix products, matmul_t(): lax.dot_general(left, right, (((0,), (0,)), ((), ())), precision=lax.Prec...  44.3 us
    dot_general x19, matrix products, matmul(): jnp.dot(left, right, preferred_element_type=jnp.float32, precision=lax.Pr...  34.1 us
    another operation x1, loops' own time, forward_block(): lax.fori_loop(0, count_nodes, advance, (pending, finished_solution))  15.5 us
    all_gather x1, waiting for transfers between devices, shapes_produce(): new = jnp.sum(jax.lax.all_gather(load, axis_name='front'), 0)  14.1 us
    another operation x1, loops' own time, backward_block(): known_rows = lax.fori_loop(0, count_nodes, retreat, known_rows)  14 us
    another operation x16, other arithmetic  12.1 us
    scatter x8, local copies, waits for them, and re-layouts, retreat(): jnp.zeros(parent_value.shape, jnp.float32).at[row_index[node_pos]]  12 us
  transfers between devices with their start and end apart: 5, of which 5 were waited for; matrix products, arithmetic and copies ran while one was open for 0% of the time, Pallas kernels for 0%

profile of v1, /device:TPU:0, one launch (start us, length us, event | category | flops | bytes accessed | tf_op | source)
XLA Modules:
  0.0 376.9 jit_solution(14664386184688474829)
XLA Ops:
  9.8 79.2 %while.59 = (s32[]{:T(128)}, f32[9,256,256]{2,1,0:T(8,128)S(1)}, f32[8,256,256]{2,1,0:T(8,128)}, s32[8]{0:T(128)S(1)}, s32[8,256]{1,0:T(8,128)}, /*index=5*/f32[...) while((s32[]{:T(128)}, f32[9,256,256]{2,1,0:T(8,128)S(1)}, ...), condition=%wide.region_3.4_spmd, body=%wide.region_0.3_spmd.sunk | while | flops 402984224 | bytes 3683810 | solution.py:57
  13.1 2.8 fusion.67
  23.0 2.8 fusion.67
  32.9 2.8 fusion.67
  42.8 2.8 fusion.67
  52.7 2.8 fusion.67
  62.6 2.8 fusion.67
  72.5 2.8 fusion.67
  82.4 2.8 fusion.67
  89.9 7.2 %all_gather.38 = f32[256,256]{1,0:T(8,128)S(1)} all-gather(f32[64,256]{1,0:T(8,128)S(1)} %copy-done.3), channel_id=1, replica_groups=mesh['leaf'=8,'front'=4] {'front'}, dimensions={0}, use_global_device_ids=true | all-gather | bytes 327680 | tf_op jit(solution)/shard_map/all_gather | solution.py:98
  97.3 6.3 %all_gather.39 = f32[256,256]{1,0:T(8,128)} all-gather(f32[64,256]{1,0:T(8,128)S(1)} %convolution_negate_fusion.1), channel_id=1, replica_groups=mesh['leaf'=8,'front'=4] {'front'}, dimensions={0}, use_global_device_ids=true | all-gather | bytes 327680 | tf_op jit(solution)/shard_map/all_gather | solution.py:102
  103.7 9.0 %reduce-scatter.2.cloned.1.call-done = f32[64,256]{1,0:T(8,128)} async-done(((f32[256,256]{1,0:T(8,128)}), f32[64,256]{1,0:T(8,128)}) %reduce-scatter.2.cloned.1.call-update) | async-done | bytes 65552 | tf_op jit(solution)/shard_map/reduce_scatter | solution.py:96
  113.5 5.8 %all_gather.42 = f32[256,256]{1,0:T(8,128)S(1)} all-gather(f32[64,256]{1,0:T(8,128)S(1)} %sub.46), channel_id=1, replica_groups=mesh['leaf'=8,'front'=4] {'front'}, dimensions={0}, use_global_device_ids=true | all-gather | bytes 327680 | tf_op jit(solution)/shard_map/all_gather | solution.py:99
  119.6 6.3 %all_gather.43 = f32[256,256]{1,0:T(8,128)} all-gather(f32[64,256]{1,0:T(8,128)S(1)} %convolution_bitcast_fusion.2), channel_id=1, replica_groups=mesh['leaf'=8,'front'=4] {'front'}, dimensions={0}, use_global_device_ids=true | all-gather | bytes 327680 | tf_op jit(solution)/shard_map/all_gather | solution.py:103
  126.0 28.4 %all-gather.9.cloned.1.call-done = f32[2048,256]{1,0:T(8,128)} async-done(((f32[256,256]{1,0:T(8,128)}), f32[2048,256]{1,0:T(8,128)}) %all-gather.9.cloned.1.call-update) | async-done | bytes 2097168 | tf_op jit(solution)/shard_map/all_gather | solution.py:11
  154.4 49.9 %all-gather.11.cloned.1.call-done = f32[2048,256]{1,0:T(8,128)} async-done(((f32[256,256]{1,0:T(8,128)}), f32[2048,256]{1,0:T(8,128)}) %all-gather.11.cloned.1.call-update) | async-done | bytes 2097168 | tf_op jit(solution)/shard_map/all_gather | solution.py:11
  207.2 57.1 %all-gather.13.cloned.1.call-done = f32[2048,256]{1,0:T(8,128)} async-done(((f32[256,256]{1,0:T(8,128)}), f32[2048,256]{1,0:T(8,128)}) %all-gather.13.cloned.1.call-update) | async-done | bytes 2097168 | tf_op jit(solution)/shard_map/all_gather | solution.py:11
  264.3 11.9 %while.61 = (s32[]{:T(128)}, f32[256,256]{1,0:T(8,128)S(1)}, s32[]{:T(128)}, f32[8,256,256]{2,1,0:T(8,128)}, f32[8,256,256]{2,1,0:T(8,128)}, /*index=5*/s32[]{:T(128)}, s32[]{:T(128)}, s32[]{:T(128)}, s32[]{:T(128)}) while((s32[]{:T(128)}, f32[256,256]{1,0:T(8,128)S(1)}, s32[]{:T(128)}, f32[8,256,256]{2,1,0:T(8,128)}, ...), condition=%wide.region_8.9_spmd, body=%wide.region_7.8_spmd.sunk | while | flops 201392128 | bytes 1574027 | solution.py:20
  277.4 14.1 %all-gather.15.cloned.1.call-done = f32[1024,256]{0,1:T(8,128)} async-done(((f32[256,256]{0,1:T(8,128)}), f32[1024,256]{0,1:T(8,128)}) %all-gather.15.cloned.1.call-update) | async-done | bytes 1048592 | tf_op jit(solution)/shard_map/all_gather | solution.py:87
  295.0 72.8 %while.62 = (s32[]{:T(128)}, f32[9,256,256]{2,1,0:T(8,128)S(1)}, f32[8,256,256]{2,1,0:T(8,128)}, f32[8,256,256]{2,1,0:T(8,128)}, f32[8,256,256]{2,1,0:T(8,128)},...) while((s32[]{:T(128)}, f32[9,256,256]{2,1,0:T(8,128)S(1)}, ...), condition=%wide.region_13.14_spmd, body=%wide.region_10.13_spmd.sunk | while | flops 402785056 | bytes 2625843 | solution.py:80
  301.9 2.2 fusion.80
  320.1 2.2 fusion.80
  338.3 2.2 fusion.80
  347.4 2.2 fusion.80
  (167 shorter events, 115.8 us)
Async XLA Ops:
  8.0 89.1 %copy-start = (f32[64,256]{1,0:T(8,128)S(1)}, f32[64,256]{1,0:T(8,128)}, u32[]{:S(2)}) copy-start(f32[64,256]{1,0:T(8,128)} %param.28) | copy-start | bytes 196612
  8.0 104.7 %reduce-scatter.2.cloned.1.call-start = ((), (), s32[]{:S(2)}) async-start(), calls=%async_computation.1 | async-start | bytes 327680 | tf_op jit(solution)/shard_map/reduce_scatter | solution.py:96
  8.1 1.7 copy-start.5
  8.1 1.7 copy-start.6
  8.1 1.7 copy-start.7
  9.8 80.1 %copy-start.3 = (f32[64,256]{1,0:T(8,128)S(1)}, f32[64,256]{1,0:T(8,128)}, u32[]{:S(2)}) copy-start(f32[64,256]{1,0:T(8,128)} %param.29) | copy-start | bytes 196612
  89.1 23.6 %copy-start.4 = (f32[64,256]{1,0:T(8,128)S(1)}, f32[64,256]{1,0:T(8,128)}, u32[]{:S(2)}) copy-start(f32[64,256]{1,0:T(8,128)} %param.27) | copy-start | bytes 196612
  89.8 64.6 %all-gather.9.cloned.1.call-start = ((), (), s32[]{:S(2)}) async-start(), calls=%async_computation.2 | async-start | bytes 2359296 | tf_op jit(solution)/shard_map/all_gather | solution.py:11
  103.7 100.7 %all-gather.11.cloned.1.call-start = ((), (), s32[]{:S(2)}) async-start(), calls=%async_computation.3 | async-start | bytes 2359296 | tf_op jit(solution)/shard_map/all_gather | solution.py:11
  125.9 138.4 %all-gather.13.cloned.1.call-start = ((), (), s32[]{:S(2)}) async-start(), calls=%async_computation.4 | async-start | bytes 2359296 | tf_op jit(solution)/shard_map/all_gather | solution.py:11
  204.4 1.0 copy-start.1
  204.4 1.0 copy-start.2
  207.1 84.4 %all-gather.15.cloned.1.call-start = ((), (), s32[]{:S(2)}) async-start(), calls=%async_computation.5 | async-start | bytes 1310720 | tf_op jit(solution)/shard_map/all_gather | solution.py:87
Sparse Core Ops, SparseCore 0:
  89.9 22.7 reduce-scatter.1
  277.5 13.9 all-gather.14
Sparse Core Ops, SparseCore 1:
  103.7 50.6 all-gather.8
  156.6 47.7 all-gather.10
  207.2 57.1 all-gather.12
